TPU v7x, 32 devices: a whole 2x2x4 slice. The times are simulated.
32 devices in a mesh: groups: 2 (over y), tok: 4 (over x, core), head: 4 (over z).
Axes of the slice: x: 2, y: 2, z: 4, core: 2. Of those that a mesh axis runs over, the one named last changes fastest.
Arguments:
- keys: bfloat16 [24576, 1280], P(('groups', 'tok'), 'head'), parts along dimension 0, may hold values from -6 to 6
- values: bfloat16 [24576, 1280], P(('groups', 'tok'), 'head'), parts along dimension 0, may hold values from -6 to 6
- rates: float32 [24576, 4], P(('groups', 'tok'), 'head'), parts along dimension 0, may hold values from 0.5 to 4
- fast_init: bfloat16 [4, 3, 320, 320], P('head'), may hold values from -6 to 6
- samples: bfloat16 [512, 5120], P('groups', 'tok'), parts along dimension 0, may hold values from -6 to 6
- w_query: bfloat16 [5120, 1280], P('tok', 'head'), may hold values from -0.078125 to 0.078125
- w_output: bfloat16 [1280, 5120], P('head', 'tok'), may hold values from -0.15625 to 0.15625
Outputs:
- mixed: bfloat16 [512, 5120], P(('groups', 'head'), 'tok'), parts along dimension 0
- fast_new: bfloat16 [8, 3, 320, 320], P(('groups', 'head')), parts along dimension 0
There are 2 independent parts, one for each index of `groups`. A program takes and returns all parts, laid end to end along the dimension named above; an argument that names none is the same for every part. Nothing has to cross between parts.
All inputs are finite; a program needn't handle non-finite values.
Results may differ from a plain program's by a relative error of at most 0.012.
Values may be sent and summed in bfloat16 or wider, within the bound.
A program may use at most 64 MiB of HBM per device.

v0:
```python
import jax
import jax.numpy as jnp
from jax import lax
from jax.sharding import PartitionSpec as P


def unit_rows(block):
    wide = block.astype(jnp.float32)
    return (wide * lax.rsqrt(jnp.sum(wide * wide, axis=-1, keepdims=True) + 1e-06)).astype(
        jnp.bfloat16
    )


def renorm(weights, gradient):
    former = weights.astype(jnp.float32)
    updated = former + gradient
    factor = jnp.sqrt(
        (jnp.mean(former * former, axis=-1, keepdims=True) + 1e-05)
        / (jnp.mean(updated * updated, axis=-1, keepdims=True) + 1e-05)
    )
    return (updated * factor).astype(jnp.bfloat16)


def shards(keys, values, rates, fast_init, samples, w_query, w_output):
    tok_count = lax.axis_size("tok")
    head_dev = fast_init.shape[0]
    head_size = fast_init.shape[2]
    token_rows = keys.shape[0]
    step_scale = float(token_rows * tok_count) ** (-0.5)
    normed = unit_rows(keys.reshape(token_rows, head_dev, head_size))
    pre_gate = jnp.einsum(
        "thd,hde->the", normed, fast_init[:, 0], preferred_element_type=jnp.float32
    )
    pre_up = jnp.einsum("thd,hde->the", normed, fast_init[:, 1], preferred_element_type=jnp.float32)
    gate_sigmoid = jax.nn.sigmoid(pre_gate)
    activated = pre_gate * gate_sigmoid
    hidden = (activated * pre_up).astype(jnp.bfloat16)
    scaled = (
        rates[:, :, None] * values.reshape(token_rows, head_dev, head_size).astype(jnp.float32)
    ).astype(jnp.bfloat16)
    hidden_grad = jnp.einsum(
        "the,hde->thd", scaled, fast_init[:, 2], preferred_element_type=jnp.float32
    )
    gate_grad = (
        hidden_grad * pre_up * gate_sigmoid * (1.0 + pre_gate * (1.0 - gate_sigmoid))
    ).astype(jnp.bfloat16)
    up_grad = (hidden_grad * activated).astype(jnp.bfloat16)
    grad_first = jnp.einsum("thd,the->hde", normed, gate_grad, preferred_element_type=jnp.float32)
    grad_second = jnp.einsum("thd,the->hde", normed, up_grad, preferred_element_type=jnp.float32)
    grad_third = jnp.einsum("thd,the->hde", hidden, scaled, preferred_element_type=jnp.float32)
    gradient = jnp.stack([grad_first, grad_second, grad_third], axis=1)
    total = lax.psum(gradient, "tok") * step_scale
    fast_new = renorm(fast_init, total)
    sample_rows = samples.shape[0] // tok_count
    queries = lax.psum_scatter(
        jnp.dot(samples, w_query, preferred_element_type=jnp.float32),
        "tok",
        scatter_dimension=0,
        tiled=True,
    )
    normed_queries = unit_rows(queries.reshape(sample_rows, head_dev, head_size))
    sample_gate = jnp.einsum(
        "shd,hde->she", normed_queries, fast_new[:, 0], preferred_element_type=jnp.float32
    )
    sample_up = jnp.einsum(
        "shd,hde->she", normed_queries, fast_new[:, 1], preferred_element_type=jnp.float32
    )
    sample_hidden = (jax.nn.silu(sample_gate) * sample_up).astype(jnp.bfloat16)
    fast_out = jnp.einsum(
        "shd,hde->she", sample_hidden, fast_new[:, 2], preferred_element_type=jnp.float32
    )
    normed_out = (
        fast_out * lax.rsqrt(jnp.mean(fast_out * fast_out, axis=-1, keepdims=True) + 1e-05)
    ).astype(jnp.bfloat16)
    normed_out = normed_out.reshape(sample_rows, head_dev * head_size)
    terms = jnp.dot(
        lax.all_gather(normed_out, "tok", axis=0, tiled=True),
        w_output,
        preferred_element_type=jnp.float32,
    )
    mixed = lax.psum_scatter(terms, "head", scatter_dimension=0, tiled=True).astype(jnp.bfloat16)
    return (mixed, fast_new)


def solution(mesh):
    return jax.shard_map(
        shards,
        mesh=mesh,
        in_specs=(
            P(("groups", "tok"), "head"),
            P(("groups", "tok"), "head"),
            P(("groups", "tok"), "head"),
            P("head", None, None, None),
            P("groups", "tok"),
            P("tok", "head"),
            P("head", "tok"),
        ),
        out_specs=(P(("groups", "head"), "tok"), P(("groups", "head"), None, None, None)),
        check_vma=False,
    )
```

profile of v0, /device:TPU:0, one launch (start us, length us, event | category | flops | bytes accessed | tf_op | source)
XLA Modules:
  0.0 139.4 jit_solution(2106379427797200033)
XLA Ops:
  7.2 2.0 %fusion = f32[3072]{0:T(1024)S(1)} fusion(bf16[3072,320]{0,1:T(8,128)(2,1)} %param.7), kind=kLoop, calls=%fused_computation.5 | loop fusion | flops 2946048 | bytes 1978368 | tf_op jit(solution)/shard_map/reduce_sum | solution.py:9
  9.3 2.9 %convolution_bitcast_fusion.1 = f32[3072,1,320]{0,2,1:T(8,128)S(1)} fusion(bf16[3072,320]{0,1:T(8,128)(2,1)} %param.7, f32[3072]{0:T(1024)S(1)} %add_rsqrt_fusion, bf16[1,3,320,320]{3,2,1,0:T(8,128)(2,1)} %param.10), kind=kOutput, calls=%fused_computation.3 | convolution fusion | flops 632094720 | bytes 6156288 | tf_op jit(solution)/shard_map/thd,hde->the/dot_general | solution.py:31
  12.3 1.3 convolution_bitcast_fusion.2
  13.5 0.3 copy-done.3
  13.8 1.2 convolution_bitcast_fusion
  15.0 1.5 %fusion.19 = f32[1,1,320,320]{3,2,1,0:T(8,128)S(1)} fusion(f32[3072,1,320]{0,2,1:T(8,128)S(1)} %convolution_bitcast_fusion, bf16[3072,320]{0,1:T(8,128)(2,1)S(1)} %copy-done.1, f32[3072]{0:T(1024)S(1)} %add_rsqrt_fusion, f32[3072,1,320]{0,2,1:T(8,128)S(1)} %convolution_bitcast_fusion.1), kind=kOutput, calls=%fused_computation.26 | convolution fusion | flops 637992960 | bytes 10252288 | tf_op jit(solution)/shard_map/thd,the->hde/dot_general | solution.py:49
  16.5 2.1 %fusion.24 = f32[1,1,320,320]{3,2,1,0:T(8,128)S(1)} fusion(f32[3072,1,320]{0,2,1:T(8,128)S(1)} %convolution_bitcast_fusion.1, f32[3072,1,320]{0,2,1:T(8,128)S(1)} %convolution_bitcast_fusion, f32[3072,1,320]{0,2,1:T(8,128)S(1)} %convolution_bitcast_fusion.2, bf16[3072,320]{0,1:T(8,128)(2,1)S(1)} %copy-done.1, f32[3072]{0:T(1024)S(1)} %add_rsqrt_fusion), kind=kOutput, calls=%fused_computation.27 | convolution fusion | flops 641925120 | bytes 14184448 | tf_op jit(solution)/shard_map/thd,the->hde/dot_general | solution.py:48
  18.6 1.4 %fusion.16 = f32[1,1,320,320]{3,2,1,0:T(8,128)S(1)} fusion(bf16[3072,320]{0,1:T(8,128)(2,1)S(1)} %copy-done.3, f32[3072]{0:T(1024)S(1)} %bitcast.98, f32[3072,1,320]{0,2,1:T(8,128)S(1)} %convolution_bitcast_fusion.2, f32[3072,1,320]{0,2,1:T(8,128)S(1)} %convolution_bitcast_fusion.1), kind=kOutput, calls=%fused_computation.25 | convolution fusion | flops 637992960 | bytes 10252288 | tf_op jit(solution)/shard_map/thd,the->hde/dot_general | solution.py:50
  20.1 1.2 pad_maximum_fusion
  21.4 0.1 copy-done.5
  21.5 0.4 copy-done.6
  21.9 1.3 fusion.54
  23.3 42.1 %all-reduce.2.cloned.1.call-done = f32[1,3,320,320]{3,2,1,0:T(8,128)} async-done(((f32[1,3,320,320]{3,2,1,0:T(8,128)}), f32[1,3,320,320]{3,2,1,0:T(8,128)}) %all-reduce.2.cloned.1.call-update) | async-done | bytes 1228816 | tf_op jit(solution)/shard_map/psum | solution.py:52
  65.4 1.8 %fusion.11 = (f32[3,320]{1,0:T(4,128)S(1)}, f32[3,320]{1,0:T(4,128)S(1)}) fusion(bf16[1,3,320,320]{3,2,1,0:T(8,128)(2,1)S(1)} %copy-done.2, f32[1,3,320,320]{3,2,1,0:T(8,128)} %all-reduce.2.cloned.1.call-done), kind=kLoop, calls=%fused_computation.21 | loop fusion | flops 2148480 | bytes 1850880 | tf_op jit(solution)/shard_map/reduce_sum | solution.py:18
  67.3 1.6 %multiply_convert_fusion.7 = bf16[1,3,320,320]{3,2,1,0:T(8,128)(2,1)S(1)} fusion(f32[1,3,320,320]{3,2,1,0:T(8,128)} %all-reduce.2.cloned.1.call-done, bf16[1,3,320,320]{3,2,1,0:T(8,128)(2,1)S(1)} %copy-done.2, f32[3,320]{1,0:T(4,128)S(1)} %fusion.49), kind=kLoop, calls=%fused_computation.23 | loop fusion | flops 1536000 | bytes 2461440 | tf_op jit(solution)/shard_map/convert_element_type | solution.py:21
  68.9 20.1 %reduce-scatter.3.cloned.1.call-done = f32[64,320]{1,0:T(8,128)} async-done(((f32[256,320]{1,0:T(8,128)}), f32[64,320]{1,0:T(8,128)}) %reduce-scatter.3.cloned.1.call-update) | async-done | bytes 81936 | tf_op jit(solution)/shard_map/reduce_scatter | solution.py:55
  88.9 1.0 multiply_reduce_fusion.2
  90.0 1.1 convolution_bitcast_fusion.5
  91.1 1.4 multiply_reduce_fusion.1
  92.5 0.1 fusion.47
  92.6 5.6 %all-gather = bf16[256,1,320]{2,0,1:T(8,128)(2,1)S(1)} all-gather(bf16[64,1,320]{2,0,1:T(8,128)(2,1)S(1)} %fusion.47), channel_id=2, replica_groups=mesh['groups'=2,'tok'=4,'head'=4] {'tok'}, dimensions={0}, use_global_device_ids=true | all-gather | bytes 204800 | tf_op jit(solution)/shard_map/all_gather | solution.py:77
  98.2 1.6 %fusion.40 = f32[256,1280]{1,0:T(8,128)} fusion(bf16[320,1280]{1,0:T(8,128)(2,1)S(1)} %copy-done, bf16[256,1,320]{2,0,1:T(8,128)(2,1)S(1)} %all-gather), kind=kOutput, calls=%fused_computation.43 | convolution fusion | flops 209715200 | bytes 2293760 | tf_op jit(solution)/shard_map/dot_general | solution.py:76
  99.8 31.4 %reduce-scatter.5.cloned.1.call-done = f32[64,1280]{1,0:T(8,128)} async-done(((f32[256,1280]{1,0:T(8,128)}), f32[64,1280]{1,0:T(8,128)}) %reduce-scatter.5.cloned.1.call-update) | async-done | bytes 327696 | tf_op jit(solution)/shard_map/reduce_scatter | solution.py:81
  131.2 1.7 %convert_element_type.60 = bf16[64,1280]{1,0:T(8,128)(2,1)} convert(f32[64,1280]{1,0:T(8,128)} %reduce-scatter.5.cloned.1.call-done) | non-fusion elementwise | flops 81920 | bytes 491520 | tf_op jit(solution)/shard_map/convert_element_type | solution.py:81
  (23 shorter events, 0.3 us)
Async XLA Ops:
  7.2 91.0 %copy-start = (bf16[320,1280]{1,0:T(8,128)(2,1)S(1)}, bf16[320,1280]{1,0:T(8,128)(2,1)}, u32[]{:S(2)}) copy-start(bf16[320,1280]{1,0:T(8,128)(2,1)} %param.13) | copy-start | bytes 2457604
  7.2 58.2 %all-reduce.2.cloned.1.call-start = ((), (), s32[]{:S(2)}) async-start(), calls=%async_computation.2 | async-start | bytes 2949120 | tf_op jit(solution)/shard_map/psum | solution.py:52
  9.2 3.0 %copy-start.1 = (bf16[3072,320]{0,1:T(8,128)(2,1)S(1)}, bf16[3072,320]{0,1:T(8,128)(2,1)}, u32[]{:S(2)}) copy-start(bf16[3072,320]{0,1:T(8,128)(2,1)} %param.7) | copy-start | bytes 5898244
  9.3 3.0 %copy-start.2 = (bf16[1,3,320,320]{3,2,1,0:T(8,128)(2,1)S(1)}, bf16[1,3,320,320]{3,2,1,0:T(8,128)(2,1)}, u32[]{:S(2)}) copy-start(bf16[1,3,320,320]{3,2,1,0:T(8,128)(2,1)} %param.10) | copy-start | bytes 1843204
  12.3 1.5 %copy-start.3 = (bf16[3072,320]{0,1:T(8,128)(2,1)S(1)}, bf16[3072,320]{0,1:T(8,128)(2,1)}, u32[]{:S(2)}) copy-start(bf16[3072,320]{0,1:T(8,128)(2,1)} %param.8) | copy-start | bytes 5898244
  12.3 1.5 %copy-start.7 = (f32[3072,1]{0,1:T(1,128)S(1)}, f32[3072,1]{0,1:T(1,128)}, u32[]{:S(2)}) copy-start(f32[3072,1]{0,1:T(1,128)} %param.9) | copy-start | bytes 36868
  20.0 1.4 %copy-start.5 = (bf16[1280,320]{0,1:T(8,128)(2,1)S(1)}, bf16[1280,320]{0,1:T(8,128)(2,1)}, u32[]{:S(2)}) copy-start(bf16[1280,320]{0,1:T(8,128)(2,1)} %param.12) | copy-start | bytes 2457604
  20.1 1.9 %copy-start.6 = (bf16[256,1280]{1,0:T(8,128)(2,1)S(1)}, bf16[256,1280]{1,0:T(8,128)(2,1)}, u32[]{:S(2)}) copy-start(bf16[256,1280]{1,0:T(8,128)(2,1)} %param.11) | copy-start | bytes 1966084
  21.3 67.6 %reduce-scatter.3.cloned.1.call-start = ((), (), s32[]{:S(2)}) async-start(), calls=%async_computation.3 | async-start | bytes 491520 | tf_op jit(solution)/shard_map/reduce_scatter | solution.py:55
  23.2 108.0 %reduce-scatter.5.cloned.1.call-start = ((), (), s32[]{:S(2)}) async-start(), calls=%async_computation.4 | async-start | bytes 1638400 | tf_op jit(solution)/shard_map/reduce_scatter | solution.py:81
  68.9 64.0 %copy-start.4 = (bf16[1,3,320,320]{3,2,1,0:T(8,128)(2,1)}, bf16[1,3,320,320]{3,2,1,0:T(8,128)(2,1)S(1)}, u32[]{:S(2)}) copy-start(bf16[1,3,320,320]{3,2,1,0:T(8,128)(2,1)S(1)} %multiply_convert_fusion.7) | copy-start | bytes 1843204
Sparse Core Ops, SparseCore 0:
  21.4 43.9 all-reduce.1
  68.0 20.8 reduce-scatter.2
  99.9 31.2 reduce-scatter.4
where the time goes:
time: 140 us; the launch traced here: 139 us
  waiting for transfers between devices  93.6 us (67%)
  matrix products  15.8 us (11%)
  between operations  13.9 us (10%)
  other arithmetic  9.47 us (7%)
  blocking collectives  5.61 us (4%)
    psum x1, waiting for transfers between devices, shards(): total = lax.psum(gradient, 'tok') * step_scale  42.1 us
    reduce_scatter x1, waiting for transfers between devices, shards(): lax.psum_scatter(terms, 'head', scatter_dimension=0, tiled=True)  31.4 us
    reduce_scatter x1, waiting for transfers between devices, shards(): lax.psum_scatter(jnp.dot(samples, w_query, preferred_element_type=jnp.flo...  20.1 us
    all_gather x1, blocking collectives, shards(): lax.all_gather(normed_out, 'tok', axis=0, tiled=True)  5.61 us
    reduce_sum x2, other arithmetic, unit_rows(): jnp.sum(wide * wide, axis=-1, keepdims=True) + 1e-06  3.02 us
    dot_general x1, matrix products, shards(): jnp.einsum('thd,hde->the', normed, fast_init[:, 0], preferred_element_typ...  2.94 us
  transfers between devices with their start and end apart: 3, of which 3 were waited for; matrix products, arithmetic and copies ran while one was open for 3% of the time, Pallas kernels for 0%

commit v1 on v0

v1 whole, which is shorter than its diff:
```python
import functools

import jax
import jax.numpy as jnp
from jax import lax
from jax.experimental import pallas as pl
from jax.experimental.pallas import tpu as pltpu
from jax.sharding import PartitionSpec as P

MESH = pl.DeviceIdType.MESH
F32 = jnp.float32
BF16 = jnp.bfloat16


def dot(a, b):
    return jnp.dot(a, b, preferred_element_type=F32)


def dot_tn(a, b):
    return lax.dot_general(a, b, (((0,), (0,)), ((), ())), preferred_element_type=F32)


def dot_nt(a, b):
    return lax.dot_general(a, b, (((1,), (1,)), ((), ())), preferred_element_type=F32)


def sigmoid(v):
    return 0.5 * jnp.tanh(0.5 * v) + 0.5


def kernel(
    n_tok, n_head, chunks, step_scale,
    keys_h, values_h, rates_h, init_h, samples_h, wq_h, wo_h,
    mixed_ref, fast_h,
    keys_v, values_v, rates_v, init_v, samples_v, wq_v, wo_v, wo_pair,
    w13, w2, acc12, acc3, crecv12, crecv3, xbuf, fnew,
    qsend, qrecv, nq, nout, nrecv, tsend, trecv,
    load_sem, chunk_sem, wo_sem, q_ssem, q_rsem, c_ssem, c_rsem,
    x_ssem, x_rsem, f_ssem, f_rsem, out_sem, n_ssem, n_rsem, t_ssem, t_rsem,
):
    t = lax.axis_index("tok")
    h = lax.axis_index("head")
    n_x = n_tok // 2
    n_pair = n_head // 2
    x = t // 2
    core = lax.rem(t, 2)
    par = lax.rem(h, 2)
    pair = h // 2
    core_peer = {"tok": 2 * x + 1 - core}
    head_peer = {"head": 2 * pair + 1 - par}
    tok_peers = [{"tok": lax.rem(t + d, n_tok)} for d in range(1, n_tok)]
    x_peers = [{"tok": 2 * lax.rem(x + d, n_x) + core} for d in range(1, n_x)]
    pair_of = [lax.rem(pair + o, n_pair) for o in range(n_pair)]
    par_peers = [{"head": 2 * pair_of[o] + par} for o in range(1, n_pair)]

    barrier = pltpu.get_barrier_semaphore()
    everyone = tok_peers + [head_peer] + par_peers
    for peer in everyone:
        pl.semaphore_signal(barrier, inc=1, device_id=peer, device_id_type=MESH)

    loads = [
        pltpu.make_async_copy(samples_h, samples_v, load_sem.at[0]),
        pltpu.make_async_copy(wq_h, wq_v, load_sem.at[1]),
        pltpu.make_async_copy(init_h.at[0], init_v, load_sem.at[2]),
    ]
    rows = keys_h.shape[0] // chunks

    def chunk_copies(i):
        at = pl.ds(pl.multiple_of(i * rows, rows), rows)
        return [
            pltpu.make_async_copy(keys_h.at[at], keys_v.at[at], chunk_sem.at[0, i]),
            pltpu.make_async_copy(values_h.at[at], values_v.at[at], chunk_sem.at[1, i]),
            pltpu.make_async_copy(rates_h.at[at], rates_v.at[at], chunk_sem.at[2, i]),
        ]

    for load in loads:
        load.start()
    for i in range(chunks):
        for c in chunk_copies(i):
            c.start()
    wo_load = pltpu.make_async_copy(wo_h, wo_v, load_sem.at[3])
    wo_load.start()

    acc12[...] = jnp.zeros_like(acc12)
    acc3[...] = jnp.zeros_like(acc3)
    w13[...] = jnp.zeros_like(w13)

    hd = fnew.shape[1]
    wide = w2.shape[0]
    half = hd // 2

    loads[0].wait()
    loads[1].wait()
    queries = dot(samples_v[...], wq_v[...])
    qsend[...] = queries.astype(BF16)

    pl.semaphore_wait(barrier, len(everyone))

    wo_swap = pltpu.make_async_remote_copy(
        src_ref=wo_h, dst_ref=wo_pair, send_sem=wo_sem.at[0], recv_sem=wo_sem.at[1],
        device_id=head_peer, device_id_type=MESH,
    )
    wo_swap.start()
    q_copies = []
    for d, peer in enumerate(tok_peers):
        q_copies.append(pltpu.make_async_remote_copy(
            src_ref=qsend, dst_ref=qrecv.at[d], send_sem=q_ssem.at[d], recv_sem=q_rsem.at[d],
            device_id=peer, device_id_type=MESH,
        ))
        q_copies[-1].start()

    loads[2].wait()
    w13[:, :hd] = init_v[0]
    w13[:, wide : wide + hd] = init_v[1]
    w2[:hd, :] = init_v[2]
    w2[hd:, :] = jnp.zeros((wide - hd, hd), BF16)

    def body(i, carry):
        for c in chunk_copies(i):
            c.wait()
        at = pl.ds(pl.multiple_of(i * rows, rows), rows)
        k = keys_v[at, :].astype(F32)
        normed = (k * lax.rsqrt(jnp.sum(k * k, axis=-1, keepdims=True) + 1e-06)).astype(BF16)
        pre = dot(normed, w13[...])
        gate, up = pre[:, :wide], pre[:, wide:]
        scaled = (rates_v[at, :] * values_v[at, :].astype(F32)).astype(BF16)
        hidden_grad = dot_nt(scaled, w2[...])
        s = sigmoid(gate)
        a = gate * s
        hidden = (a * up).astype(BF16)
        gate_grad = (hidden_grad * up * (s + a * (1.0 - s))).astype(BF16)
        up_grad = (hidden_grad * a).astype(BF16)
        acc12[...] += dot_tn(normed, jnp.concatenate([gate_grad, up_grad], axis=1))
        acc3[...] += dot_tn(hidden[:, :hd], scaled)
        return carry

    lax.fori_loop(0, chunks, body, 0)

    theirs = pl.ds(pl.multiple_of(half * (1 - core), half), half)
    mine = pl.ds(pl.multiple_of(half * core, half), half)
    c_copies = [
        pltpu.make_async_remote_copy(
            src_ref=acc12.at[theirs], dst_ref=crecv12, send_sem=c_ssem.at[0],
            recv_sem=c_rsem.at[0], device_id=core_peer, device_id_type=MESH,
        ),
        pltpu.make_async_remote_copy(
            src_ref=acc3.at[theirs], dst_ref=crecv3, send_sem=c_ssem.at[1],
            recv_sem=c_rsem.at[1], device_id=core_peer, device_id_type=MESH,
        ),
    ]
    for c in c_copies:
        c.start()

    for c in q_copies:
        c.wait_recv()
    for d in range(n_tok - 1):
        queries = queries + qrecv[d].astype(F32)
    nq[...] = (
        queries * lax.rsqrt(jnp.sum(queries * queries, axis=-1, keepdims=True) + 1e-06)
    ).astype(BF16)

    c_copies[0].wait_recv()
    s12 = acc12[mine, :] + crecv12[...]
    xbuf[x, 0] = s12[:, :hd].astype(BF16)
    xbuf[x, 1] = s12[:, wide : wide + hd].astype(BF16)
    c_copies[1].wait_recv()
    xbuf[x, 2] = (acc3[mine, :] + crecv3[...]).astype(BF16)
    x_copies = []
    for d, peer in enumerate(x_peers):
        x_copies.append(pltpu.make_async_remote_copy(
            src_ref=xbuf.at[x], dst_ref=xbuf.at[x], send_sem=x_ssem.at[d], recv_sem=x_rsem.at[d],
            device_id=peer, device_id_type=MESH,
        ))
        x_copies[-1].start()
    for c in x_copies:
        c.wait_recv()

    f_copies = []
    for m in range(3):
        total = xbuf[0, m].astype(F32)
        for j in range(1, n_x):
            total = total + xbuf[j, m].astype(F32)
        former = init_v[m, mine, :].astype(F32)
        updated = former + total * step_scale
        factor = jnp.sqrt(
            (jnp.mean(former * former, axis=-1, keepdims=True) + 1e-05)
            / (jnp.mean(updated * updated, axis=-1, keepdims=True) + 1e-05)
        )
        fnew[m, mine, :] = (updated * factor).astype(BF16)
        f_copies.append(pltpu.make_async_remote_copy(
            src_ref=fnew.at[m, mine], dst_ref=fnew.at[m, mine], send_sem=f_ssem.at[m],
            recv_sem=f_rsem.at[m], device_id=core_peer, device_id_type=MESH,
        ))
        f_copies[-1].start()

    normed_q = nq[...]
    f_copies[0].wait_recv()
    gate = dot(normed_q, fnew[0])
    f_copies[1].wait_recv()
    up = dot(normed_q, fnew[1])
    sample_hidden = (gate * sigmoid(gate) * up).astype(BF16)
    f_copies[2].wait_recv()
    out_copy = pltpu.make_async_copy(fnew, fast_h.at[0], out_sem)
    out_copy.start()
    fast_out = dot(sample_hidden, fnew[2])
    normed_out = (
        fast_out * lax.rsqrt(jnp.mean(fast_out * fast_out, axis=-1, keepdims=True) + 1e-05)
    ).astype(BF16)
    block = nout.shape[1]
    for d in range(n_head):
        nout[d] = normed_out[d * block : (d + 1) * block]

    n_copies = []
    for j in range(n_pair):
        n_copies.append(pltpu.make_async_remote_copy(
            src_ref=nout.at[2 * j + 1 - par], dst_ref=nrecv.at[j], send_sem=n_ssem.at[j],
            recv_sem=n_rsem.at[j], device_id=head_peer, device_id_type=MESH,
        ))
        n_copies[-1].start()
    wo_load.wait()
    wo_swap.wait_recv()
    for c in n_copies:
        c.wait_recv()

    def terms(o):
        j = pair_of[o]
        return dot(nout[2 * j + par], wo_v[...]) + dot(nrecv[j], wo_pair[...])

    t_copies = []
    for o in range(1, n_pair):
        tsend[o - 1] = terms(o).astype(BF16)
        t_copies.append(pltpu.make_async_remote_copy(
            src_ref=tsend.at[o - 1], dst_ref=trecv.at[o - 1], send_sem=t_ssem.at[o - 1],
            recv_sem=t_rsem.at[o - 1], device_id=par_peers[o - 1], device_id_type=MESH,
        ))
        t_copies[-1].start()
    mixed = terms(0)
    for o, c in enumerate(t_copies):
        c.wait_recv()
        mixed = mixed + trecv[o].astype(F32)
    mixed_ref[...] = mixed.astype(BF16)

    out_copy.wait()
    for c in [wo_swap] + q_copies + c_copies + x_copies + f_copies + n_copies + t_copies:
        c.wait_send()


def shards(n_tok, n_head, keys, values, rates, fast_init, samples, w_query, w_output):
    tokens = keys.shape[0]
    hd = fast_init.shape[2]
    wide = -(-hd // 128) * 128
    chunks = 4
    srows = samples.shape[0]
    block = srows // n_head
    cols = w_output.shape[1]
    n_x, n_pair = n_tok // 2, n_head // 2
    dma = pltpu.SemaphoreType.DMA
    others = max(n_pair - 1, 1)
    body = functools.partial(
        kernel, n_tok, n_head, chunks, float(tokens * n_tok) ** (-0.5)
    )
    anywhere = pl.BlockSpec(memory_space=pl.ANY)
    return pl.pallas_call(
        body,
        out_shape=(
            jax.ShapeDtypeStruct((block, cols), BF16),
            jax.ShapeDtypeStruct((1, 3, hd, hd), BF16),
        ),
        in_specs=[anywhere] * 7,
        out_specs=(pl.BlockSpec(memory_space=pltpu.VMEM), anywhere),
        scratch_shapes=[
            pltpu.VMEM(keys.shape, BF16),
            pltpu.VMEM(values.shape, BF16),
            pltpu.VMEM(rates.shape, F32),
            pltpu.VMEM((3, hd, hd), BF16),
            pltpu.VMEM(samples.shape, BF16),
            pltpu.VMEM(w_query.shape, BF16),
            pltpu.VMEM(w_output.shape, BF16),
            pltpu.VMEM(w_output.shape, BF16),
            pltpu.VMEM((hd, 2 * wide), BF16),
            pltpu.VMEM((wide, hd), BF16),
            pltpu.VMEM((hd, 2 * wide), F32),
            pltpu.VMEM((hd, hd), F32),
            pltpu.VMEM((hd // 2, 2 * wide), F32),
            pltpu.VMEM((hd // 2, hd), F32),
            pltpu.VMEM((n_x, 3, hd // 2, hd), BF16),
            pltpu.VMEM((3, hd, hd), BF16),
            pltpu.VMEM((srows, hd), BF16),
            pltpu.VMEM((n_tok - 1, srows, hd), BF16),
            pltpu.VMEM((srows, hd), BF16),
            pltpu.VMEM((n_head, block, hd), BF16),
            pltpu.VMEM((n_pair, block, hd), BF16),
            pltpu.VMEM((others, block, cols), BF16),
            pltpu.VMEM((others, block, cols), BF16),
            dma((4,)),
            dma((3, chunks)),
            dma((2,)),
            dma((n_tok - 1,)),
            dma((n_tok - 1,)),
            dma((2,)),
            dma((2,)),
            dma((max(n_x - 1, 1),)),
            dma((max(n_x - 1, 1),)),
            dma((3,)),
            dma((3,)),
            dma(()),
            dma((n_pair,)),
            dma((n_pair,)),
            dma((others,)),
            dma((others,)),
        ],
        compiler_params=pltpu.CompilerParams(
            collective_id=0, has_side_effects=True, vmem_limit_bytes=56 << 20
        ),
    )(keys, values, rates, fast_init, samples, w_query, w_output)


def solution(mesh):
    return jax.shard_map(
        functools.partial(shards, mesh.shape["tok"], mesh.shape["head"]),
        mesh=mesh,
        in_specs=(
            P(("groups", "tok"), "head"),
            P(("groups", "tok"), "head"),
            P(("groups", "tok"), "head"),
            P("head", None, None, None),
            P("groups", "tok"),
            P("tok", "head"),
            P("head", "tok"),
        ),
        out_specs=(P(("groups", "head"), "tok"), P(("groups", "head"), None, None, None)),
        check_vma=False,
    )
```

time: 140 us -> 60.4 us (0.43)
  waiting for transfers between devices: 93.6 us -> 0 us
  Pallas kernels: 0 us -> 44.5 us
  matrix products: 15.8 us -> 0 us
  local copies, waits for them, and re-layouts: 0.87 us -> 14.9 us
  between operations: 13.9 us -> 0.65 us
  other arithmetic: 9.47 us -> 0 us
  blocking collectives: 5.61 us -> 0 us
    reduce_scatter x2 -> x0, waiting for transfers between devices: 51.4 us -> none  [the longest x1 31.4 us: shards(): lax.psum_scatter(terms, 'head', scatter_dimension=0, tiled=True)]
    pallas_call x0 -> x1, Pallas kernels: none -> 44.5 us  [shards(): pl.pallas_call(body, out_shape=(jax.ShapeDtypeStruct((block, cols), BF16)...]
    psum x1 -> x0, waiting for transfers between devices: 42.1 us -> none  [shards(): total = lax.psum(gradient, 'tok') * step_scale]
    dot_general x10 -> x0, matrix products: 15.8 us -> none  [the longest x1 2.94 us: shards(): jnp.einsum('thd,hde->the', normed, fast_init[:, 0], preferred_element_typ...]
    unnamed x16 -> x8, local copies, waits for them, and re-layouts: 0.87 us -> 14.9 us
    all_gather x1 -> x0, blocking collectives: 5.61 us -> none  [shards(): lax.all_gather(normed_out, 'tok', axis=0, tiled=True)]
    reduce_sum x3 -> x0, other arithmetic: 4.86 us -> none  [the longest x2 3.02 us: unit_rows(): jnp.sum(wide * wide, axis=-1, keepdims=True) + 1e-06]
    convert_element_type x3 -> x0, other arithmetic: 3.37 us -> none  [the longest x1 1.66 us: shards(): lax.psum_scatter(terms, 'head', scatter_dimension=0, tiled=True)]
  transfers between devices with their start and end apart: 3 -> 0, of which waited for: 3 -> 0; matrix products, arithmetic and copies ran while one was open for 3% -> 0% of each run, Pallas kernels for 0% -> 0%
where the time goes in v1:
time: 60.4 us; the launch traced here: 60.1 us
  Pallas kernels  44.5 us (74%)
  local copies, waits for them, and re-layouts  14.9 us (25%)
  between operations  0.65 us (1%)
    pallas_call x1, Pallas kernels, shards(): pl.pallas_call(body, out_shape=(jax.ShapeDtypeStruct((block, cols), BF16)...  44.5 us
    unnamed x8, local copies, waits for them, and re-layouts  14.9 us

profile of v1, /device:TPU:0, one launch (start us, length us, event | category | flops | bytes accessed | tf_op | source)
XLA Modules:
  0.0 60.1 jit_solution(11445802773079285505)
XLA Ops:
  0.6 0.0 copy-start
  0.6 2.4 %copy.12.wq_h = bf16[1280,320]{1,0:T(8,128)(2,1)} copy(bf16[1280,320]{0,1:T(8,128)(2,1)} %param.12) | data formatting | bytes 1638400 | tf_op args[5]
  3.0 2.4 %copy.11.rates_h = f32[3072,1]{1,0:T(8,128)} copy(f32[3072,1]{0,1:T(1,128)} %param.9) | data formatting | bytes 24576 | tf_op args[2]
  5.4 0.0 copy-done
  5.4 2.4 %copy.9.keys_h = bf16[3072,320]{1,0:T(8,128)(2,1)} copy(bf16[3072,320]{0,1:T(8,128)(2,1)S(1)} %copy-done) | data formatting | bytes 3932160 | tf_op args[0]
  7.8 4.1 %copy.10.values_h = bf16[3072,320]{1,0:T(8,128)(2,1)} copy(bf16[3072,320]{0,1:T(8,128)(2,1)} %param.8) | data formatting | bytes 3932160 | tf_op args[1]
  11.9 44.5 %shard_map.86 = (bf16[64,1280]{1,0:T(8,128)(2,1)}, bf16[1,3,320,320]{3,2,1,0:T(8,128)(2,1)}) custom-call(bf16[3072,320]{1,0:T(8,128)(2,1)} %copy.9.keys_h, bf16[3072,320]{1,0:T(8,128)(2,1)} %copy.10.values_h, f32[3072,1]{1,0:T(8,128)} %copy.11.rates_h, bf16[1,3,320,320]{3,2,1,0:T(8,128)(2,1)} %init_h.1, bf16[256,1280]{1,0:T(8,128)(2,1)} %samples_h.1, ...), custom_call_target="tpu_custom_call" | custom-call | tf_op jit(solution)/shard_map/pallas_call | solution.py:263
  56.4 1.6 %copy.15 = bf16[64,1280]{1,0:T(8,128)(2,1)} copy(bf16[64,1280]{1,0:T(8,128)(2,1)} %get-tuple-element.4) | data formatting | bytes 327680
  58.0 2.1 %copy.16 = bf16[1,3,320,320]{3,2,1,0:T(8,128)(2,1)} copy(bf16[1,3,320,320]{3,2,1,0:T(8,128)(2,1)} %get-tuple-element.5) | data formatting | bytes 1228800
Async XLA Ops:
  0.6 4.8 %copy-start = (bf16[3072,320]{0,1:T(8,128)(2,1)S(1)}, bf16[3072,320]{0,1:T(8,128)(2,1)}, u32[]{:S(2)}) copy-start(bf16[3072,320]{0,1:T(8,128)(2,1)} %param.7) | copy-start | bytes 5898244

commit v2 on v1

v2 whole, which is shorter than its diff:
```python
import functools

import jax
import jax.numpy as jnp
from jax import lax
from jax.experimental import pallas as pl
from jax.experimental.pallas import tpu as pltpu
from jax.sharding import PartitionSpec as P

MESH = pl.DeviceIdType.MESH
F32 = jnp.float32
BF16 = jnp.bfloat16


def dot(a, b):
    return jnp.dot(a, b, preferred_element_type=F32)


def dot_tn(a, b):
    return lax.dot_general(a, b, (((0,), (0,)), ((), ())), preferred_element_type=F32)


def dot_nt(a, b):
    return lax.dot_general(a, b, (((1,), (1,)), ((), ())), preferred_element_type=F32)


def sigmoid(v):
    return 0.5 * jnp.tanh(0.5 * v) + 0.5


def pack(block):
    r, hd = block.shape
    full = hd // 128
    parts = [block[:, 128 * i : 128 * (i + 1)] for i in range(full)]
    tail = block[:, 128 * full :]
    parts.append(jnp.concatenate([tail[: r // 2], tail[r // 2 :]], axis=1))
    return parts


def unpack(rows_of, r, hd):
    full = hd // 128
    parts = [rows_of(i * r, r) for i in range(full)]
    tail = rows_of(full * r, r // 2)
    parts.append(jnp.concatenate([tail[:, :64], tail[:, 64:]], axis=0))
    return jnp.concatenate(parts, axis=1)


def kernel(
    n_tok, n_head, chunks, step_scale,
    keys_h, values_h, rates_h, init_h, samples_h, wq_h, wo_h,
    mixed_ref, fast_h,
    keys_v, values_v, rates_v, init_v, samples_v, wq_v, wo_v, wo_pair,
    w13, normed_v, scaled_v, hidden_v, gate_v, up_v, acc, crecv, xbuf, fnew,
    qbuf, qpeer, qx, nq, nout, nrecv, tsend, trecv,
    load_sem, chunk_sem, wo_sem, q_sem, qx_ssem, qx_rsem, c_ssem, c_rsem,
    x_ssem, x_rsem, f_ssem, f_rsem, out_sem, n_ssem, n_rsem, t_ssem, t_rsem,
):
    t = lax.axis_index("tok")
    h = lax.axis_index("head")
    n_x = n_tok // 2
    n_pair = n_head // 2
    x = t // 2
    core = lax.rem(t, 2)
    par = lax.rem(h, 2)
    pair = h // 2
    core_peer = {"tok": 2 * x + 1 - core}
    head_peer = {"head": 2 * pair + 1 - par}
    x_peers = [{"tok": 2 * lax.rem(x + d, n_x) + core} for d in range(1, n_x)]
    pair_of = [lax.rem(pair + o, n_pair) for o in range(n_pair)]
    par_peers = [{"head": 2 * pair_of[o] + par} for o in range(1, n_pair)]

    barrier = pltpu.get_barrier_semaphore()
    everyone = [core_peer, head_peer] + x_peers + par_peers
    for peer in everyone:
        pl.semaphore_signal(barrier, inc=1, device_id=peer, device_id_type=MESH)

    sends = []

    def send(src, dst, ssem, rsem, peer):
        copy = pltpu.make_async_remote_copy(
            src_ref=src, dst_ref=dst, send_sem=ssem, recv_sem=rsem,
            device_id=peer, device_id_type=MESH,
        )
        copy.start()
        sends.append(copy)
        return copy

    rows = keys_h.shape[1] // chunks

    def chunk_copies(i):
        at = pl.ds(i * rows, rows)
        return [
            pltpu.make_async_copy(keys_h.at[:, at], keys_v.at[:, at], chunk_sem.at[0, i]),
            pltpu.make_async_copy(values_h.at[:, at], values_v.at[:, at], chunk_sem.at[1, i]),
        ]

    loads = [
        pltpu.make_async_copy(samples_h, samples_v, load_sem.at[0]),
        pltpu.make_async_copy(wq_h, wq_v, load_sem.at[1]),
        pltpu.make_async_copy(init_h.at[0], init_v, load_sem.at[2]),
        pltpu.make_async_copy(rates_h, rates_v, load_sem.at[3]),
        pltpu.make_async_copy(wo_h, wo_v, load_sem.at[4]),
    ]
    for load in loads[:4]:
        load.start()
    for i in range(chunks):
        for c in chunk_copies(i):
            c.start()
    loads[4].start()

    hd = fnew.shape[1]
    half = hd // 2
    qrows = nq.shape[1]

    loads[0].wait()
    loads[1].wait()
    queries = dot_nt(samples_v[...], wq_v[...])
    qbuf[0] = queries[:qrows]
    qbuf[1] = queries[qrows:]

    pl.semaphore_wait(barrier, len(everyone))

    q_core = send(qbuf.at[1 - core], qpeer, q_sem.at[0], q_sem.at[1], core_peer)
    wo_swap = send(wo_h, wo_pair, wo_sem.at[0], wo_sem.at[1], head_peer)

    loads[2].wait()
    w13[:hd] = init_v[0].T
    w13[hd:] = init_v[1].T
    loads[3].wait()

    q_x = []
    q_last = None
    for i in range(chunks):
        for c in chunk_copies(i):
            c.wait()
        at = pl.ds(i * rows, rows)
        k = keys_v[:, at].astype(F32)
        normed = (k * lax.rsqrt(jnp.sum(k * k, axis=0, keepdims=True) + 1e-06)).astype(BF16)
        normed_v[:, at] = normed
        pre = dot(w13[...], normed)
        gate, up = pre[:hd], pre[hd:]
        scaled = (rates_v[:, at] * values_v[:, at].astype(F32)).astype(BF16)
        scaled_v[:, at] = scaled
        hidden_grad = dot(init_v[2], scaled)
        s = sigmoid(gate)
        a = gate * s
        hidden_v[:, at] = (a * up).astype(BF16)
        gate_v[:, at] = (hidden_grad * up * (s + a * (1.0 - s))).astype(BF16)
        up_v[:, at] = (hidden_grad * a).astype(BF16)
        if i == 0:
            q_core.wait_recv()
            qx[x] = qbuf[core] + qpeer[...]
            for d, peer in enumerate(x_peers):
                q_x.append(send(qx.at[x], qx.at[x], qx_ssem.at[d], qx_rsem.at[d], peer))
        if i == chunks - 1:
            for c in q_x:
                c.wait_recv()
            queries = qx[0]
            for j in range(1, n_x):
                queries = queries + qx[j]
            nq[core] = (
                queries
                * lax.rsqrt(jnp.sum(queries * queries, axis=-1, keepdims=True) + 1e-06)
            ).astype(BF16)
            q_last = send(nq.at[core], nq.at[core], q_sem.at[2], q_sem.at[3], core_peer)

    factors = ((normed_v, gate_v), (normed_v, up_v), (hidden_v, scaled_v))
    theirs = pl.ds(pl.multiple_of(half * (1 - core), half), half)
    mine = pl.ds(pl.multiple_of(half * core, half), half)
    c_copies, x_copies = [], []

    def chip_sum(m):
        c_copies[m].wait_recv()
        total = (acc[m, mine, :] + crecv[m]).astype(BF16)
        at = 0
        for part in pack(total):
            xbuf[m, x, at : at + part.shape[0], :] = part
            at += part.shape[0]
        x_copies.append([
            send(xbuf.at[m, x], xbuf.at[m, x], x_ssem.at[m, d], x_rsem.at[m, d], peer)
            for d, peer in enumerate(x_peers)
        ])

    for m in range(3):
        acc[m] = dot_nt(factors[m][0][...], factors[m][1][...])
        c_copies.append(
            send(acc.at[m, theirs], crecv.at[m], c_ssem.at[m], c_rsem.at[m], core_peer)
        )
        if m:
            chip_sum(m - 1)
    chip_sum(2)

    f_copies = []
    for m in range(3):
        for c in x_copies[m]:
            c.wait_recv()
        total = unpack(lambda at, r: xbuf[m, 0, at : at + r, :].astype(F32), half, hd)
        for j in range(1, n_x):
            total = total + unpack(
                lambda at, r: xbuf[m, j, at : at + r, :].astype(F32), half, hd
            )
        former = init_v[m, mine, :].astype(F32)
        updated = former + total * step_scale
        factor = jnp.sqrt(
            (jnp.mean(former * former, axis=-1, keepdims=True) + 1e-05)
            / (jnp.mean(updated * updated, axis=-1, keepdims=True) + 1e-05)
        )
        fnew[m, mine, :] = (updated * factor).astype(BF16)
        f_copies.append(send(
            fnew.at[m, mine], fnew.at[m, mine], f_ssem.at[m], f_rsem.at[m], core_peer
        ))
        if m == 0:
            q_last.wait_recv()
            normed_q = nq[...].reshape(2 * qrows, hd)
        if m == 1:
            f_copies[0].wait_recv()
            gate = dot(normed_q, fnew[0])
            gate = gate * sigmoid(gate)
        if m == 2:
            f_copies[1].wait_recv()
            sample_hidden = (gate * dot(normed_q, fnew[1])).astype(BF16)
    f_copies[2].wait_recv()
    out_copy = pltpu.make_async_copy(fnew, fast_h.at[0], out_sem)
    out_copy.start()
    fast_out = dot(sample_hidden, fnew[2])
    normed_out = (
        fast_out * lax.rsqrt(jnp.mean(fast_out * fast_out, axis=-1, keepdims=True) + 1e-05)
    ).astype(BF16)
    block = nout.shape[1]
    for d in range(n_head):
        nout[d] = normed_out[d * block : (d + 1) * block]

    n_copies = [
        send(nout.at[2 * j + 1 - par], nrecv.at[j], n_ssem.at[j], n_rsem.at[j], head_peer)
        for j in range(n_pair)
    ]
    loads[4].wait()
    wo_swap.wait_recv()
    own = [dot(nout[2 * pair_of[o] + par], wo_v[...]) for o in range(n_pair)]
    for c in n_copies:
        c.wait_recv()
    t_copies = []
    for o in range(1, n_pair):
        tsend[o - 1] = (own[o] + dot(nrecv[pair_of[o]], wo_pair[...])).astype(BF16)
        t_copies.append(send(
            tsend.at[o - 1], trecv.at[o - 1], t_ssem.at[o - 1], t_rsem.at[o - 1],
            par_peers[o - 1],
        ))
    mixed = own[0] + dot(nrecv[pair], wo_pair[...])
    for o, c in enumerate(t_copies):
        c.wait_recv()
        mixed = mixed + trecv[o].astype(F32)
    mixed_ref[...] = mixed.astype(BF16)

    out_copy.wait()
    for c in sends:
        c.wait_send()


def copy_out(mixed_ref, fast_ref, mixed_out, fast_out, sem):
    copies = [
        pltpu.make_async_copy(mixed_ref, mixed_out, sem.at[0]),
        pltpu.make_async_copy(fast_ref, fast_out, sem.at[1]),
    ]
    for c in copies:
        c.start()
    for c in copies:
        c.wait()


def shards(n_tok, n_head, keys, values, rates, fast_init, samples, w_query, w_output):
    tokens = keys.shape[0]
    hd = fast_init.shape[2]
    chunks = 4
    srows = samples.shape[0]
    block = srows // n_head
    cols = w_output.shape[1]
    n_x, n_pair = n_tok // 2, n_head // 2
    dma = pltpu.SemaphoreType.DMA
    others = max(n_pair - 1, 1)
    other_x = max(n_x - 1, 1)
    body = functools.partial(
        kernel, n_tok, n_head, chunks, float(tokens * n_tok) ** (-0.5)
    )
    anywhere = pl.BlockSpec(memory_space=pl.ANY)
    vmem = pltpu.VMEM
    packed = (hd // 2) * hd // 128
    outs = (
        jax.ShapeDtypeStruct((block, cols), BF16),
        jax.ShapeDtypeStruct((1, 3, hd, hd), BF16),
    )
    mixed, fast_new = pl.pallas_call(
        body,
        out_shape=outs,
        in_specs=[anywhere] * 7,
        out_specs=(pl.BlockSpec(memory_space=pltpu.VMEM), anywhere),
        scratch_shapes=[
            vmem((hd, tokens), BF16),
            vmem((hd, tokens), BF16),
            vmem((1, tokens), F32),
            vmem((3, hd, hd), BF16),
            vmem(samples.shape, BF16),
            vmem((hd, w_query.shape[0]), BF16),
            vmem(w_output.shape, BF16),
            vmem(w_output.shape, BF16),
            vmem((2 * hd, hd), BF16),
            vmem((hd, tokens), BF16),
            vmem((hd, tokens), BF16),
            vmem((hd, tokens), BF16),
            vmem((hd, tokens), BF16),
            vmem((hd, tokens), BF16),
            vmem((3, hd, hd), F32),
            vmem((3, hd // 2, hd), F32),
            vmem((3, n_x, packed, 128), BF16),
            vmem((3, hd, hd), BF16),
            vmem((2, srows // 2, hd), F32),
            vmem((srows // 2, hd), F32),
            vmem((n_x, srows // 2, hd), F32),
            vmem((2, srows // 2, hd), BF16),
            vmem((n_head, block, hd), BF16),
            vmem((n_pair, block, hd), BF16),
            vmem((others, block, cols), BF16),
            vmem((others, block, cols), BF16),
            dma((5,)),
            dma((2, chunks)),
            dma((2,)),
            dma((4,)),
            dma((other_x,)),
            dma((other_x,)),
            dma((3,)),
            dma((3,)),
            dma((3, other_x)),
            dma((3, other_x)),
            dma((3,)),
            dma((3,)),
            dma(()),
            dma((n_pair,)),
            dma((n_pair,)),
            dma((others,)),
            dma((others,)),
        ],
        compiler_params=pltpu.CompilerParams(
            collective_id=0, has_side_effects=True, vmem_limit_bytes=56 << 20
        ),
    )(keys.T, values.T, rates.T, fast_init, samples, w_query.T, w_output)
    return pl.pallas_call(
        copy_out,
        out_shape=outs,
        in_specs=[anywhere] * 2,
        out_specs=(anywhere, anywhere),
        scratch_shapes=[dma((2,))],
    )(mixed, fast_new)


def solution(mesh):
    return jax.shard_map(
        functools.partial(shards, mesh.shape["tok"], mesh.shape["head"]),
        mesh=mesh,
        in_specs=(
            P(("groups", "tok"), "head"),
            P(("groups", "tok"), "head"),
            P(("groups", "tok"), "head"),
            P("head", None, None, None),
            P("groups", "tok"),
            P("tok", "head"),
            P("head", "tok"),
        ),
        out_specs=(P(("groups", "head"), "tok"), P(("groups", "head"), None, None, None)),
        check_vma=False,
    )
```

time: 60.4 us -> 71.3 us (1.18)
  Pallas kernels: 44.5 us -> 70.5 us
  local copies, waits for them, and re-layouts: 14.9 us -> 0 us
    pallas_call x1 -> x2, Pallas kernels: 44.5 us -> 70.5 us  [the longest x1 42.1 us: shards(): pl.pallas_call(body, out_shape=outs, in_specs=[anywhere] * 7, out_specs=(...]
    unnamed x8 -> x0, local copies, waits for them, and re-layouts: 14.9 us -> none
where the time goes in v2:
time: 71.3 us; the launch traced here: 71.2 us
  Pallas kernels  70.5 us (99%)
    pallas_call x1, Pallas kernels, shards(): pl.pallas_call(body, out_shape=outs, in_specs=[anywhere] * 7, out_specs=(...  42.1 us
    pallas_call x1, Pallas kernels, shards(): pl.pallas_call(copy_out, out_shape=outs, in_specs=[anywhere] * 2, out_spe...  28.4 us

profile of v2, /device:TPU:0, one launch (start us, length us, event | category | flops | bytes accessed | tf_op | source)
XLA Modules:
  0.0 71.2 jit_solution(18407653312031117369)
XLA Ops:
  0.6 42.1 %shard_map.86 = (bf16[64,1280]{1,0:T(8,128)(2,1)}, bf16[1,3,320,320]{3,2,1,0:T(8,128)(2,1)}) custom-call(bf16[320,3072]{1,0:T(8,128)(2,1)} %bitcast.4, bf16[320,3072]{1,0:T(8,128)(2,1)} %bitcast.5, f32[1,3072]{1,0:T(1,128)} %bitcast.7, bf16[1,3,320,320]{3,2,1,0:T(8,128)(2,1)} %init_h.1, bf16[256,1280]{1,0:T(8,128)(2,1)} %samples_h.1, ...), custom_call_target="tpu_custom_call" | custom-call | tf_op jit(solution)/shard_map/pallas_call | solution.py:292
  42.8 28.4 %shard_map.87 = (bf16[64,1280]{1,0:T(8,128)(2,1)}, bf16[1,3,320,320]{3,2,1,0:T(8,128)(2,1)}) custom-call(bf16[64,1280]{1,0:T(8,128)(2,1)} %get-tuple-element.4.mixed_ref, bf16[1,3,320,320]{3,2,1,0:T(8,128)(2,1)} %get-tuple-element.5.fast_ref), custom_call_target="tpu_custom_call" | custom-call | tf_op jit(solution)/shard_map/pallas_call | solution.py:346

commit v3 on v2

--- a/solution.py
+++ b/solution.py
@@ -257,15 +257,9 @@
         c.wait_send()
 
 
-def copy_out(mixed_ref, fast_ref, mixed_out, fast_out, sem):
-    copies = [
-        pltpu.make_async_copy(mixed_ref, mixed_out, sem.at[0]),
-        pltpu.make_async_copy(fast_ref, fast_out, sem.at[1]),
-    ]
-    for c in copies:
-        c.start()
-    for c in copies:
-        c.wait()
+def copy_out(mixed_ref, fast_ref, mixed_out, fast_out):
+    mixed_out[...] = mixed_ref[...]
+    fast_out[...] = fast_ref[...]
 
 
 def shards(n_tok, n_head, keys, values, rates, fast_init, samples, w_query, w_output):
@@ -283,6 +277,7 @@
         kernel, n_tok, n_head, chunks, float(tokens * n_tok) ** (-0.5)
     )
     anywhere = pl.BlockSpec(memory_space=pl.ANY)
+    whole = pl.BlockSpec(memory_space=pltpu.VMEM)
     vmem = pltpu.VMEM
     packed = (hd // 2) * hd // 128
     outs = (
@@ -346,9 +341,8 @@
     return pl.pallas_call(
         copy_out,
         out_shape=outs,
-        in_specs=[anywhere] * 2,
-        out_specs=(anywhere, anywhere),
-        scratch_shapes=[dma((2,))],
+        in_specs=[whole] * 2,
+        out_specs=(whole, whole),
     )(mixed, fast_new)
 
 

time: 71.3 us -> 45.1 us (0.63)
  Pallas kernels: 70.5 us -> 44.3 us
    pallas_call x1, Pallas kernels: 28.4 us -> 2.15 us  [shards(): pl.pallas_call(copy_out, out_shape=outs, in_specs=[whole] * 2, out_specs=...]
where the time goes in v3:
time: 45.1 us; the launch traced here: 44.9 us
  Pallas kernels  44.3 us (98%)
  between operations  0.64 us (1%)
    pallas_call x1, Pallas kernels, shards(): pl.pallas_call(body, out_shape=outs, in_specs=[anywhere] * 7, out_specs=(...  42.1 us
    pallas_call x1, Pallas kernels, shards(): pl.pallas_call(copy_out, out_shape=outs, in_specs=[whole] * 2, out_specs=...  2.15 us

profile of v3, /device:TPU:0, one launch (start us, length us, event | category | flops | bytes accessed | tf_op | source)
XLA Modules:
  0.0 44.9 jit_solution(18335865757345817128)
XLA Ops:
  0.6 42.1 %shard_map.86 = (bf16[64,1280]{1,0:T(8,128)(2,1)}, bf16[1,3,320,320]{3,2,1,0:T(8,128)(2,1)}) custom-call(bf16[320,3072]{1,0:T(8,128)(2,1)} %bitcast.4, bf16[320,3072]{1,0:T(8,128)(2,1)} %bitcast.5, f32[1,3072]{1,0:T(1,128)} %bitcast.7, bf16[1,3,320,320]{3,2,1,0:T(8,128)(2,1)} %init_h.1, bf16[256,1280]{1,0:T(8,128)(2,1)} %samples_h.1, ...), custom_call_target="tpu_custom_call" | custom-call | tf_op jit(solution)/shard_map/pallas_call | solution.py:287
  42.8 2.1 %shard_map.87 = (bf16[64,1280]{1,0:T(8,128)(2,1)}, bf16[1,3,320,320]{3,2,1,0:T(8,128)(2,1)}) custom-call(bf16[64,1280]{1,0:T(8,128)(2,1)} %get-tuple-element.4.mixed_ref, bf16[1,3,320,320]{3,2,1,0:T(8,128)(2,1)} %get-tuple-element.5.fast_ref), custom_call_target="tpu_custom_call" | custom-call | tf_op jit(solution)/shard_map/pallas_call | solution.py:341

commit v4 on v3

--- a/solution.py
+++ b/solution.py
@@ -110,7 +110,8 @@
 
     hd = fnew.shape[1]
     half = hd // 2
-    qrows = nq.shape[1]
+    qrows = qpeer.shape[0]
+    group = nq.shape[2]
 
     loads[0].wait()
     loads[1].wait()
@@ -158,10 +159,12 @@
             queries = qx[0]
             for j in range(1, n_x):
                 queries = queries + qx[j]
-            nq[core] = (
+            normed_q = (
                 queries
                 * lax.rsqrt(jnp.sum(queries * queries, axis=-1, keepdims=True) + 1e-06)
             ).astype(BF16)
+            for j in range(nq.shape[1]):
+                nq[core, j] = normed_q[j * group : (j + 1) * group]
             q_last = send(nq.at[core], nq.at[core], q_sem.at[2], q_sem.at[3], core_peer)
 
     factors = ((normed_v, gate_v), (normed_v, up_v), (hidden_v, scaled_v))
@@ -211,46 +214,59 @@
         ))
         if m == 0:
             q_last.wait_recv()
-            normed_q = nq[...].reshape(2 * qrows, hd)
-        if m == 1:
-            f_copies[0].wait_recv()
-            gate = dot(normed_q, fnew[0])
-            gate = gate * sigmoid(gate)
-        if m == 2:
-            f_copies[1].wait_recv()
-            sample_hidden = (gate * dot(normed_q, fnew[1])).astype(BF16)
+
+    order = list(range(1, n_pair)) + [0]
+    per_half = nq.shape[1]
+    block = group // 2
+    gates, hiddens = [], []
+    normed_q = [nq[pair_of[o] // per_half, lax.rem(pair_of[o], per_half)] for o in order]
+    f_copies[0].wait_recv()
+    for rows_q in normed_q:
+        gate = dot(rows_q, fnew[0])
+        gates.append(gate * sigmoid(gate))
+    f_copies[1].wait_recv()
+    for gate, rows_q in zip(gates, normed_q):
+        hiddens.append((gate * dot(rows_q, fnew[1])).astype(BF16))
     f_copies[2].wait_recv()
     out_copy = pltpu.make_async_copy(fnew, fast_h.at[0], out_sem)
     out_copy.start()
-    fast_out = dot(sample_hidden, fnew[2])
-    normed_out = (
-        fast_out * lax.rsqrt(jnp.mean(fast_out * fast_out, axis=-1, keepdims=True) + 1e-05)
-    ).astype(BF16)
-    block = nout.shape[1]
-    for d in range(n_head):
-        nout[d] = normed_out[d * block : (d + 1) * block]
-
-    n_copies = [
-        send(nout.at[2 * j + 1 - par], nrecv.at[j], n_ssem.at[j], n_rsem.at[j], head_peer)
-        for j in range(n_pair)
-    ]
+    n_copies = {}
+    for o, sample_hidden in zip(order, hiddens):
+        fast_out = dot(sample_hidden, fnew[2])
+        normed_out = (
+            fast_out * lax.rsqrt(jnp.mean(fast_out * fast_out, axis=-1, keepdims=True) + 1e-05)
+        ).astype(BF16)
+        nout[o, 0] = normed_out[:block]
+        nout[o, 1] = normed_out[block:]
+        n_copies[o] = send(
+            nout.at[o, 1 - par], nrecv.at[o], n_ssem.at[o], n_rsem.at[o], head_peer
+        )
+
     loads[4].wait()
     wo_swap.wait_recv()
-    own = [dot(nout[2 * pair_of[o] + par], wo_v[...]) for o in range(n_pair)]
-    for c in n_copies:
-        c.wait_recv()
-    t_copies = []
+    parts = tsend.shape[1]
+    width = tsend.shape[3]
+
+    def terms(o, p):
+        at = slice(p * width, (p + 1) * width)
+        return dot(nout[o, par], wo_v[:, at]) + dot(nrecv[o], wo_pair[:, at])
+
+    t_copies = {}
     for o in range(1, n_pair):
-        tsend[o - 1] = (own[o] + dot(nrecv[pair_of[o]], wo_pair[...])).astype(BF16)
-        t_copies.append(send(
-            tsend.at[o - 1], trecv.at[o - 1], t_ssem.at[o - 1], t_rsem.at[o - 1],
-            par_peers[o - 1],
-        ))
-    mixed = own[0] + dot(nrecv[pair], wo_pair[...])
-    for o, c in enumerate(t_copies):
-        c.wait_recv()
-        mixed = mixed + trecv[o].astype(F32)
-    mixed_ref[...] = mixed.astype(BF16)
+        n_copies[o].wait_recv()
+        for p in range(parts):
+            tsend[o - 1, p] = terms(o, p).astype(BF16)
+            t_copies[o, p] = send(
+                tsend.at[o - 1, p], trecv.at[o - 1, p], t_ssem.at[o - 1, p],
+                t_rsem.at[o - 1, p], par_peers[o - 1],
+            )
+    n_copies[0].wait_recv()
+    mixed = [terms(0, p) for p in range(parts)]
+    for p in range(parts):
+        for o in range(1, n_pair):
+            t_copies[o, p].wait_recv()
+            mixed[p] = mixed[p] + trecv[o - 1, p].astype(F32)
+        mixed_ref[:, p * width : (p + 1) * width] = mixed[p].astype(BF16)
 
     out_copy.wait()
     for c in sends:
@@ -272,6 +288,7 @@
     n_x, n_pair = n_tok // 2, n_head // 2
     dma = pltpu.SemaphoreType.DMA
     others = max(n_pair - 1, 1)
+    parts = cols // 256 if cols % 256 == 0 else 1
     other_x = max(n_x - 1, 1)
     body = functools.partial(
         kernel, n_tok, n_head, chunks, float(tokens * n_tok) ** (-0.5)
@@ -311,11 +328,11 @@
             vmem((2, srows // 2, hd), F32),
             vmem((srows // 2, hd), F32),
             vmem((n_x, srows // 2, hd), F32),
-            vmem((2, srows // 2, hd), BF16),
-            vmem((n_head, block, hd), BF16),
+            vmem((2, n_pair // 2, 2 * block, hd), BF16),
+            vmem((n_pair, 2, block, hd), BF16),
             vmem((n_pair, block, hd), BF16),
-            vmem((others, block, cols), BF16),
-            vmem((others, block, cols), BF16),
+            vmem((others, parts, block, cols // parts), BF16),
+            vmem((others, parts, block, cols // parts), BF16),
             dma((5,)),
             dma((2, chunks)),
             dma((2,)),
@@ -331,8 +348,8 @@
             dma(()),
             dma((n_pair,)),
             dma((n_pair,)),
-            dma((others,)),
-            dma((others,)),
+            dma((others, parts)),
+            dma((others, parts)),
         ],
         compiler_params=pltpu.CompilerParams(
             collective_id=0, has_side_effects=True, vmem_limit_bytes=56 << 20

time: 45.1 us -> 43.7 us (0.969)
  Pallas kernels: 44.3 us -> 42.9 us
    pallas_call x1, Pallas kernels: 42.1 us -> 40.8 us  [shards(): pl.pallas_call(body, out_shape=outs, in_specs=[anywhere] * 7, out_specs=(...]
where the time goes in v4:
time: 43.7 us; the launch traced here: 43.6 us
  Pallas kernels  42.9 us (98%)
  between operations  0.64 us (1%)
    pallas_call x1, Pallas kernels, shards(): pl.pallas_call(body, out_shape=outs, in_specs=[anywhere] * 7, out_specs=(...  40.8 us
    pallas_call x1, Pallas kernels, shards(): pl.pallas_call(copy_out, out_shape=outs, in_specs=[whole] * 2, out_specs=...  2.15 us

profile of v4, /device:TPU:0, one launch (start us, length us, event | category | flops | bytes accessed | tf_op | source)
XLA Modules:
  0.0 43.6 jit_solution(6154258573036198599)
XLA Ops:
  0.6 40.8 %shard_map.86 = (bf16[64,1280]{1,0:T(8,128)(2,1)}, bf16[1,3,320,320]{3,2,1,0:T(8,128)(2,1)}) custom-call(bf16[320,3072]{1,0:T(8,128)(2,1)} %bitcast.4, bf16[320,3072]{1,0:T(8,128)(2,1)} %bitcast.5, f32[1,3072]{1,0:T(1,128)} %bitcast.7, bf16[1,3,320,320]{3,2,1,0:T(8,128)(2,1)} %init_h.1, bf16[256,1280]{1,0:T(8,128)(2,1)} %samples_h.1, ...), custom_call_target="tpu_custom_call" | custom-call | tf_op jit(solution)/shard_map/pallas_call | solution.py:304
  41.4 2.1 %shard_map.87 = (bf16[64,1280]{1,0:T(8,128)(2,1)}, bf16[1,3,320,320]{3,2,1,0:T(8,128)(2,1)}) custom-call(bf16[64,1280]{1,0:T(8,128)(2,1)} %get-tuple-element.4.mixed_ref, bf16[1,3,320,320]{3,2,1,0:T(8,128)(2,1)} %get-tuple-element.5.fast_ref), custom_call_target="tpu_custom_call" | custom-call | tf_op jit(solution)/shard_map/pallas_call | solution.py:358

commit v5 on v4

--- a/solution.py
+++ b/solution.py
@@ -273,15 +273,24 @@
         c.wait_send()
 
 
-def copy_out(mixed_ref, fast_ref, mixed_out, fast_out):
-    mixed_out[...] = mixed_ref[...]
-    fast_out[...] = fast_ref[...]
+def copy_out(mixed_ref, fast_ref, mixed_out, fast_out, mixed_v, fast_v, sem):
+    ways = [(mixed_ref, mixed_v, mixed_out)]
+    ways += [(fast_ref.at[0, m], fast_v.at[m], fast_out.at[0, m]) for m in range(3)]
+    loads = [pltpu.make_async_copy(w[0], w[1], sem.at[0, i]) for i, w in enumerate(ways)]
+    stores = [pltpu.make_async_copy(w[1], w[2], sem.at[1, i]) for i, w in enumerate(ways)]
+    for c in loads:
+        c.start()
+    for load, store in zip(loads, stores):
+        load.wait()
+        store.start()
+    for c in stores:
+        c.wait()
 
 
 def shards(n_tok, n_head, keys, values, rates, fast_init, samples, w_query, w_output):
     tokens = keys.shape[0]
     hd = fast_init.shape[2]
-    chunks = 4
+    chunks = 3
     srows = samples.shape[0]
     block = srows // n_head
     cols = w_output.shape[1]
@@ -294,7 +303,6 @@
         kernel, n_tok, n_head, chunks, float(tokens * n_tok) ** (-0.5)
     )
     anywhere = pl.BlockSpec(memory_space=pl.ANY)
-    whole = pl.BlockSpec(memory_space=pltpu.VMEM)
     vmem = pltpu.VMEM
     packed = (hd // 2) * hd // 128
     outs = (
@@ -358,8 +366,9 @@
     return pl.pallas_call(
         copy_out,
         out_shape=outs,
-        in_specs=[whole] * 2,
-        out_specs=(whole, whole),
+        in_specs=[anywhere] * 2,
+        out_specs=(anywhere, anywhere),
+        scratch_shapes=[vmem((block, cols), BF16), vmem((3, hd, hd), BF16), dma((2, 4))],
     )(mixed, fast_new)
 
 

time: 43.7 us -> 42.7 us (0.977)
  Pallas kernels: 42.9 us -> 41.9 us
    pallas_call x1, Pallas kernels: 40.8 us -> 39.9 us  [shards(): pl.pallas_call(body, out_shape=outs, in_specs=[anywhere] * 7, out_specs=(...]
where the time goes in v5:
time: 42.7 us; the launch traced here: 42.6 us
  Pallas kernels  41.9 us (98%)
  between operations  0.64 us (1%)
    pallas_call x1, Pallas kernels, shards(): pl.pallas_call(body, out_shape=outs, in_specs=[anywhere] * 7, out_specs=(...  39.9 us
    pallas_call x1, Pallas kernels, shards(): pl.pallas_call(copy_out, out_shape=outs, in_specs=[anywhere] * 2, out_spe...  2.03 us

profile of v5, /device:TPU:0, one launch (start us, length us, event | category | flops | bytes accessed | tf_op | source)
XLA Modules:
  0.0 42.6 jit_solution(11502904572117693426)
XLA Ops:
  0.6 39.9 %shard_map.86 = (bf16[64,1280]{1,0:T(8,128)(2,1)}, bf16[1,3,320,320]{3,2,1,0:T(8,128)(2,1)}) custom-call(bf16[320,3072]{1,0:T(8,128)(2,1)} %bitcast.4, bf16[320,3072]{1,0:T(8,128)(2,1)} %bitcast.5, f32[1,3072]{1,0:T(1,128)} %bitcast.7, bf16[1,3,320,320]{3,2,1,0:T(8,128)(2,1)} %init_h.1, bf16[256,1280]{1,0:T(8,128)(2,1)} %samples_h.1, ...), custom_call_target="tpu_custom_call" | custom-call | tf_op jit(solution)/shard_map/pallas_call | solution.py:312
  40.5 2.0 %shard_map.87 = (bf16[64,1280]{1,0:T(8,128)(2,1)}, bf16[1,3,320,320]{3,2,1,0:T(8,128)(2,1)}) custom-call(bf16[64,1280]{1,0:T(8,128)(2,1)} %get-tuple-element.4.mixed_ref, bf16[1,3,320,320]{3,2,1,0:T(8,128)(2,1)} %get-tuple-element.5.fast_ref), custom_call_target="tpu_custom_call" | custom-call | tf_op jit(solution)/shard_map/pallas_call | solution.py:366

commit v6 on v5

--- a/solution.py
+++ b/solution.py
@@ -290,7 +290,7 @@
 def shards(n_tok, n_head, keys, values, rates, fast_init, samples, w_query, w_output):
     tokens = keys.shape[0]
     hd = fast_init.shape[2]
-    chunks = 3
+    chunks = 2
     srows = samples.shape[0]
     block = srows // n_head
     cols = w_output.shape[1]

time: 42.7 us -> 43.2 us (1.012)
  Pallas kernels: 41.9 us -> 42.4 us
    pallas_call x1, Pallas kernels: 39.9 us -> 40.4 us  [shards(): pl.pallas_call(body, out_shape=outs, in_specs=[anywhere] * 7, out_specs=(...]
where the time goes in v6:
time: 43.2 us; the launch traced here: 43 us
  Pallas kernels  42.4 us (98%)
  between operations  0.64 us (1%)
    pallas_call x1, Pallas kernels, shards(): pl.pallas_call(body, out_shape=outs, in_specs=[anywhere] * 7, out_specs=(...  40.4 us
    pallas_call x1, Pallas kernels, shards(): pl.pallas_call(copy_out, out_shape=outs, in_specs=[anywhere] * 2, out_spe...  2.03 us

profile of v6, /device:TPU:0, one launch (start us, length us, event | category | flops | bytes accessed | tf_op | source)
XLA Modules:
  0.0 43.0 jit_solution(2640757782802990115)
XLA Ops:
  0.6 40.4 %shard_map.86 = (bf16[64,1280]{1,0:T(8,128)(2,1)}, bf16[1,3,320,320]{3,2,1,0:T(8,128)(2,1)}) custom-call(bf16[320,3072]{1,0:T(8,128)(2,1)} %bitcast.4, bf16[320,3072]{1,0:T(8,128)(2,1)} %bitcast.5, f32[1,3072]{1,0:T(1,128)} %bitcast.7, bf16[1,3,320,320]{3,2,1,0:T(8,128)(2,1)} %init_h.1, bf16[256,1280]{1,0:T(8,128)(2,1)} %samples_h.1, ...), custom_call_target="tpu_custom_call" | custom-call | tf_op jit(solution)/shard_map/pallas_call | solution.py:312
  41.0 2.0 %shard_map.87 = (bf16[64,1280]{1,0:T(8,128)(2,1)}, bf16[1,3,320,320]{3,2,1,0:T(8,128)(2,1)}) custom-call(bf16[64,1280]{1,0:T(8,128)(2,1)} %get-tuple-element.4.mixed_ref, bf16[1,3,320,320]{3,2,1,0:T(8,128)(2,1)} %get-tuple-element.5.fast_ref), custom_call_target="tpu_custom_call" | custom-call | tf_op jit(solution)/shard_map/pallas_call | solution.py:366
